TPU v7x, 32 devices: a whole 2x2x4 slice. The times are simulated.
32 devices in a mesh: ens: 16 (over z, y, x), slab: 2 (over core).
Axes of the slice: x: 2, y: 2, z: 4, core: 2. Of those that a mesh axis runs over, the one named last changes fastest.
Arguments:
- ensemble: float32 [16, 3, 128, 768], P('ens', None, 'slab'), may hold values from -6 to 6
- perturbation: float32 [16, 3, 128, 768], P('ens', None, 'slab'), may hold values from -6 to 6
- ancestors: int32 [16], P('ens'), may hold values from 0 to 15
- bathymetry: int32 [128, 768], replicated, may hold values from 50 to 200
Outputs:
- analysis: float32 [16, 3, 128, 768], P('ens', None, 'slab')
Inputs may be any that keep to these rules, and one draw needn't show every extreme that they name: `ancestors`: each entry names the old particle that a new particle copies.
All inputs are finite; a program needn't handle non-finite values.
Results may differ from a plain program's by a relative error of at most 0.00002.
Values sent between devices are 32-bit elements; how exact they have to be, the bound alone decides.
A program may use at most 128 MiB of HBM per device.

v0:
```python
import functools

import jax
import jax.numpy as jnp
from jax import lax
from jax.experimental import pallas as pl
from jax.experimental.pallas import tpu as pltpu
from jax.sharding import PartitionSpec as P

STEPS = 3
MESH = pl.DeviceIdType.MESH
STRIP = 8
LANES = 128


RATIO = 0.3
TURNING = 0.03
JITTER = 0.5


def padded(cells, sides, width):
    for axis, dim in sides:
        count = lax.axis_size(axis)
        ends = count - 1
        head = lax.slice_in_dim(cells, 0, width, axis=dim)
        tail = lax.slice_in_dim(cells, cells.shape[dim] - width, cells.shape[dim], axis=dim)
        cells = jnp.concatenate(
            [
                lax.ppermute(tail, axis, [(i, (i + 1) % count) for i in range(ends)]),
                cells,
                lax.ppermute(head, axis, [((i + 1) % count, i) for i in range(ends)]),
            ],
            axis=dim,
        )
    return cells


def eastward_difference(field):
    return (jnp.roll(field, -1, -1) - jnp.roll(field, 1, -1)) * 0.5


def step_rows(height, east_vel, north_vel, ocean_floor, inside):
    flux_east = ocean_floor * east_vel
    flux_north = ocean_floor * north_vel
    height_next = height[1:-1] - RATIO * (
        eastward_difference(flux_east[1:-1]) + (flux_north[2:] - flux_north[:-2]) * 0.5
    )
    height_next = jnp.where(inside[1:-1], height_next, 0.0)
    east_next = (
        east_vel[2:-2] - RATIO * eastward_difference(height_next[1:-1]) + TURNING * north_vel[2:-2]
    )
    north_next = (
        north_vel[2:-2]
        - RATIO * (height_next[2:] - height_next[:-2]) * 0.5
        - TURNING * east_vel[2:-2]
    )
    kept = inside[2:-2]
    return (height_next[1:-1], jnp.where(kept, east_next, 0.0), jnp.where(kept, north_next, 0.0))


def edge_rows(members, depth):
    return jnp.stack(
        [jnp.concatenate([member[:depth], member[-depth:]], axis=0) for member in members]
    )


def attach_rims(members, rims, depth):
    return [
        jnp.concatenate([rims[k, :depth], members[k], rims[k, 3 * depth :]], axis=0)
        for k in range(len(members))
    ]


def pick_rows(portion, lineage):
    return jnp.take(portion, lineage, axis=0, mode="clip")


def shards(ensemble, perturbation, ancestors, bathymetry):
    row_count = ensemble.shape[2]
    col_count = ensemble.shape[3]
    total_rows = bathymetry.shape[0]
    first_row = lax.axis_index("slab") * row_count
    widest = 2 * STEPS
    seabed_all = jnp.pad(bathymetry.astype(jnp.float32) * 0.01, ((widest, widest), (0, 0)))
    members = [ensemble[0, 0], ensemble[0, 1], ensemble[0, 2]]
    ocean_floor = lax.dynamic_slice_in_dim(seabed_all, first_row + widest - 2, row_count + 2 * 2, 0)
    global_row = first_row - 2 + jnp.arange(row_count + 2 * 2, dtype=jnp.int32)
    inside = ((global_row >= 0) & (global_row < total_rows))[:, None]
    ocean_floor, inside = (ocean_floor, inside)
    for substep in range(STEPS):
        rims = padded(edge_rows(members, 2), (("slab", 1),), 2)
        widened = attach_rims(members, rims, 2)
        members = list(step_rows(widened[0], widened[1], widened[2], ocean_floor, inside))
    noise = [perturbation[0, 0], perturbation[0, 1], perturbation[0, 2]]
    noise_rims = padded(edge_rows(noise, 1), (("slab", 1),), 1)
    bordered = attach_rims(noise, noise_rims, 1)
    smoothed = jnp.stack(
        [
            (
                4.0 * cell[1:-1]
                + cell[2:]
                + cell[:-2]
                + jnp.roll(cell[1:-1], 1, -1)
                + jnp.roll(cell[1:-1], -1, -1)
            )
            * 0.125
            for cell in bordered
        ]
    )
    lineage = lax.all_gather(ancestors, "ens", axis=0, tiled=True)
    flattened = jnp.stack(members).reshape(1, 3, row_count * col_count)
    pieces = lax.all_to_all(flattened, "ens", split_axis=2, concat_axis=0, tiled=True)
    picked = pick_rows(pieces, lineage)
    returned = lax.all_to_all(picked, "ens", split_axis=0, concat_axis=2, tiled=True)
    selected_parents = returned.reshape(1, 3, row_count, col_count)
    return selected_parents + JITTER * smoothed[None]


def whole_wait(ref, sem):
    pltpu.make_async_copy(ref, ref, sem).wait()


def cycle_kernel(
    n, pair, rows, cols,
    ens_ref, pert_ref, anc_ref, bath_ref, out_ref,
    state, noise, sb, seam, seam_sb, bath_v, pieces0, pieces1, pieces2, picked, res, lin_v, lin_s,
    halo_send, halo_recv, lin_send, lin_recv, lin_local, loads,
    a_send, a_recv, b_send, b_recv,
):
    me = lax.axis_index("ens")
    s = lax.axis_index("slab")
    plane = pair * pair
    line = n // plane
    hubs = 2 * plane
    base = (line // 2 - 1) * plane
    z = me // plane
    y = me // pair % pair
    x = me % pair
    inward = 1 - 2 * (z // (line // 2))
    hub = jnp.logical_and(me >= base, me < base + hubs)
    pieces = (pieces0, pieces1, pieces2)
    top = STRIP
    bottom = STRIP + rows
    barrier = pltpu.get_barrier_semaphore()

    def on(level, k):
        return (level * pair + (y + k // pair) % pair) * pair + (x + k % pair) % pair

    @pl.when(hub)
    def _():
        def greet(t, carry):
            to = lax.rem(me + 1 + t, n)
            pl.semaphore_signal(barrier, inc=1, device_id={"ens": to}, device_id_type=MESH)
            return carry

        lax.fori_loop(0, n - 1, greet, 0)

    pl.semaphore_signal(barrier, inc=1, device_id={"slab": 1 - s}, device_id_type=MESH)

    inner = pl.multiple_of((1 - s) * (rows - 2 * STRIP), STRIP)
    fills = [
        pltpu.make_async_copy(src, dst, loads.at[i])
        for i, (src, dst) in enumerate(
            (
                (bath_ref.at[pl.ds(pl.multiple_of(s * (rows - STRIP), STRIP), rows + STRIP)], bath_v),
                (ens_ref, state.at[:, pl.ds(top, rows)]),
                (
                    ens_ref.at[:, pl.ds(inner, 2 * STRIP)],
                    seam.at[:, pl.ds(pl.multiple_of(s * STRIP, STRIP), 2 * STRIP)],
                ),
                (pert_ref, noise.at[:, pl.ds(top, rows)]),
            )
        )
    ]
    for fill in fills:
        fill.start()

    lin_v[me] = jnp.full((1, LANES), anc_ref[0], jnp.int32)
    zeros = jnp.zeros((STRIP, cols), jnp.float32)
    for r in (0, bottom):
        sb[r : r + STRIP] = zeros
        for f in range(3):
            state[f, r : r + STRIP] = zeros
    fills[0].wait()
    for r in range(0, rows, STRIP):
        depth = bath_v[pl.ds(pl.multiple_of(s * STRIP + r, STRIP), STRIP)]
        sb[top + r : top + r + STRIP] = depth.astype(jnp.float32) * 0.01
    for r in range(0, 3 * STRIP, STRIP):
        depth = bath_v[pl.ds(pl.multiple_of((1 - s) * (rows - 2 * STRIP) + r, STRIP), STRIP)]
        seam_sb[r : r + STRIP] = depth.astype(jnp.float32) * 0.01
    fills[1].wait()
    fills[2].wait()

    def east(x):
        return (pltpu.roll(x, cols - 1, 1) - pltpu.roll(x, 1, 1)) * 0.5

    def shifted(ref, r, by):
        if 0 <= r + by <= ref.shape[0] - STRIP:
            return ref[r + by : r + by + STRIP]
        return pltpu.roll(ref[r : r + STRIP], -by % STRIP, 0)

    def heights(cells, floor, r):
        here = slice(r, r + STRIP)
        v = cells.at[2]
        northward = shifted(floor, r, 1) * shifted(v, r, 1) - shifted(floor, r, -1) * shifted(v, r, -1)
        eastward = east(floor[here] * cells[1, here])
        cells[0, here] = cells[0, here] - RATIO * (eastward + northward * 0.5)

    def velocities(cells, r):
        here = slice(r, r + STRIP)
        u = cells[1, here]
        v = cells[2, here]
        h = cells.at[0]
        cells[1, here] = u - RATIO * east(h[here]) + TURNING * v
        northward = (shifted(h, r, 1) - shifted(h, r, -1)) * 0.5
        cells[2, here] = v - RATIO * northward - TURNING * u

    for step in range(STEPS):
        for r in range(top, bottom, STRIP):
            heights(state, sb, r)
        for r in range(top, bottom, STRIP):
            velocities(state, r)

    edge = pl.multiple_of((1 - s) * (rows - STRIP), STRIP)

    def strip(ref, f, q, offset):
        return ref.at[f, pl.ds(pl.multiple_of(offset + (q + s * (hubs - 1 - 2 * q)) * STRIP, STRIP), STRIP)]

    def deliver(f, to):
        pltpu.make_async_remote_copy(
            src_ref=strip(state, f, to - base, top),
            dst_ref=pieces[f].at[me],
            send_sem=a_send.at[f],
            recv_sem=a_recv.at[f],
            device_id={"ens": to},
            device_id_type=MESH,
        ).start()

    def keep(f):
        pltpu.make_async_copy(strip(state, f, me - base, top), pieces[f].at[me], a_recv.at[f]).start()

    def tell(to):
        pltpu.make_async_remote_copy(
            src_ref=lin_v.at[me],
            dst_ref=lin_v.at[me],
            send_sem=lin_send,
            recv_sem=lin_recv,
            device_id={"ens": to},
            device_id_type=MESH,
        ).start()

    side = line // 2 - 1 + z // (line // 2)
    targets = [on(side + inward, k) for k in reversed(range(plane))]
    targets += [on(side, k) for k in reversed(range(plane))]
    last_hub = base + hubs - 1

    def away(f):
        for to in targets[:-1]:
            pl.when(to != last_hub)(lambda to=to: deliver(f, to))
        to = targets[-1]
        pl.when(jnp.logical_and(jnp.logical_not(hub), to != last_hub))(lambda: deliver(f, to))
        pl.when(jnp.logical_and(hub, to != last_hub))(lambda: keep(f))

    def seamed(f):
        pl.when(me != last_hub)(lambda: deliver(f, last_hub))
        pl.when(me == last_hub)(lambda: keep(f))

    pl.semaphore_wait(barrier, hubs + 1 - hub.astype(jnp.int32))
    halos = []
    for i, (src, dst, row) in enumerate(
        ((ens_ref, seam, s * 2 * STRIP), (pert_ref, noise, s * (rows + STRIP)))
    ):
        copy = pltpu.make_async_remote_copy(
            src_ref=src.at[:, pl.ds(edge, STRIP)],
            dst_ref=dst.at[:, pl.ds(pl.multiple_of(row, STRIP), STRIP)],
            send_sem=halo_send.at[i],
            recv_sem=halo_recv.at[i],
            device_id={"slab": 1 - s},
            device_id_type=MESH,
        )
        copy.start()
        halos.append(copy)
    for to in targets[:-1]:
        tell(to)
    pl.when(jnp.logical_not(hub))(lambda: tell(targets[-1]))
    away(0)
    halos[0].wait()
    for step in range(STEPS):
        last = step == STEPS - 1
        for r in range(0, 3 * STRIP, STRIP):
            heights(seam, seam_sb, r)
        for r in range(STRIP, 2 * STRIP, STRIP) if last else range(0, 3 * STRIP, STRIP):
            velocities(seam, r)
    for f in range(3):
        state[f, pl.ds(pl.multiple_of(top + edge, STRIP), STRIP)] = seam[f, STRIP : 2 * STRIP]

    seamed(0)
    for f in (1, 2):
        away(f)
        seamed(f)

    wall = pl.multiple_of(s * (rows + STRIP), STRIP)
    for f in range(3):
        noise[f, pl.ds(wall, STRIP)] = zeros
    fills[3].wait()
    halos[1].wait()
    for f in range(3):
        for r in range(top, bottom, STRIP):
            p = noise[f, r : r + STRIP]
            around = noise[f, r + 1 : r + 1 + STRIP] + noise[f, r - 1 : r - 1 + STRIP]
            total = 4.0 * p + around + pltpu.roll(p, 1, 1) + pltpu.roll(p, cols - 1, 1)
            out_ref[f, r - top : r - top + STRIP] = total * 0.125 * JITTER

    order = [t for t in range(line // 2, -(line // 2), -1) if t] + [0]
    spots = [(t, k) for t in order for k in reversed(range(plane))][: n - 1]

    def serve():
        whole_wait(lin_v.at[pl.ds(0, n - 1)], lin_recv)
        fetch = pltpu.make_async_copy(lin_v, lin_s, lin_local)
        fetch.start()
        fetch.wait()

        def reply(f, i):
            t, k = spots[i]
            to = on(z + t * inward, k)
            picked[f, i] = pieces[f][lin_s[to, 0, 0]]
            pltpu.make_async_remote_copy(
                src_ref=picked.at[f, i],
                dst_ref=strip(res, f, me - base, 0),
                send_sem=b_send.at[f],
                recv_sem=b_recv.at[f],
                device_id={"ens": to},
                device_id_type=MESH,
            ).start()

        for stage in range(3 + line // 2 - 1):
            if stage < 3:
                whole_wait(pieces[stage], a_recv.at[stage])
            for i, (t, k) in enumerate(spots):
                f = stage - max(line // 2 - t, 0) if t > 0 else stage
                if 0 <= f < 3:
                    reply(f, i)
            if stage < 3:
                picked[stage, n - 1] = pieces[stage][lin_s[me, 0, 0]]
                pltpu.make_async_copy(
                    picked.at[stage, n - 1], strip(res, stage, me - base, 0), b_recv.at[stage]
                ).start()

    pl.when(hub)(serve)

    for f in range(3):
        whole_wait(res.at[f], b_recv.at[f])
        for r in range(0, rows, STRIP):
            out_ref[f, r : r + STRIP] = res[f, r : r + STRIP] + out_ref[f, r : r + STRIP]

    @pl.when(hub)
    def _():
        whole_wait(lin_v.at[pl.ds(0, hubs - 1)], lin_send)
        for f in range(3):
            whole_wait(pieces[f].at[pl.ds(0, hubs - 1)], a_send.at[f])
            whole_wait(picked.at[f, pl.ds(0, n - 1)], b_send.at[f])

    @pl.when(jnp.logical_not(hub))
    def _():
        whole_wait(lin_v.at[pl.ds(0, hubs)], lin_send)
        for f in range(3):
            whole_wait(pieces[f].at[pl.ds(0, hubs)], a_send.at[f])


def cycle(n, pair, ensemble, perturbation, ancestors, bathymetry):
    rows, cols = ensemble.shape[2:]
    tall = rows + 2 * STRIP
    f32 = jnp.float32
    vmem = pl.BlockSpec(memory_space=pltpu.VMEM)
    hbm = pl.BlockSpec(memory_space=pltpu.HBM)
    dma = pltpu.SemaphoreType.DMA
    held = [
        pltpu.with_memory_space_constraint(x, pltpu.HBM)
        for x in (ensemble[0], perturbation[0], bathymetry)
    ]
    result = pl.pallas_call(
        functools.partial(cycle_kernel, n, pair, rows, cols),
        out_shape=jax.ShapeDtypeStruct((3, rows, cols), f32),
        in_specs=[hbm, hbm, pl.BlockSpec(memory_space=pltpu.SMEM), hbm],
        out_specs=vmem,
        scratch_shapes=[
            pltpu.VMEM((3, tall, cols), f32),
            pltpu.VMEM((3, tall, cols), f32),
            pltpu.VMEM((tall, cols), f32),
            pltpu.VMEM((3, 3 * STRIP, cols), f32),
            pltpu.VMEM((3 * STRIP, cols), f32),
            pltpu.VMEM((rows + STRIP, cols), jnp.int32),
            pltpu.VMEM((n, STRIP, cols), f32),
            pltpu.VMEM((n, STRIP, cols), f32),
            pltpu.VMEM((n, STRIP, cols), f32),
            pltpu.VMEM((3, n, STRIP, cols), f32),
            pltpu.VMEM((3, rows, cols), f32),
            pltpu.VMEM((n, 1, LANES), jnp.int32),
            pltpu.SMEM((n, 1, LANES), jnp.int32),
            dma((2,)), dma((2,)), dma(()), dma(()), dma(()), dma((4,)),
            dma((3,)), dma((3,)), dma((3,)), dma((3,)),
        ],
        compiler_params=pltpu.CompilerParams(collective_id=0, has_side_effects=True, vmem_limit_bytes=24 << 20),
        name="cycle",
    )(*held[:2], ancestors, held[2])
    return result[None]


def fits(mesh, ensemble):
    n, slabs = mesh.shape["ens"], mesh.shape["slab"]
    plane = slabs * slabs
    rows, cols = ensemble.shape[2] // slabs, ensemble.shape[3]
    if slabs != 2 or ensemble.shape[0] != n or n != plane * plane:
        return False
    return rows == 2 * plane * STRIP and cols % LANES == 0


def solution(mesh):
    in_specs = (P("ens", None, "slab", None), P("ens", None, "slab", None), P("ens"), P())
    out_specs = P("ens", None, "slab", None)

    def run(ensemble, perturbation, ancestors, bathymetry):
        body = functools.partial(cycle, mesh.shape["ens"], mesh.shape["slab"]) if fits(mesh, ensemble) else shards
        mapped = jax.shard_map(body, mesh=mesh, in_specs=in_specs, out_specs=out_specs, check_vma=False)
        return mapped(ensemble, perturbation, ancestors, bathymetry)

    return run
```

profile of v0, /device:TPU:8, one launch (start us, length us, event | category | flops | bytes accessed | tf_op | source)
XLA Modules:
  0.0 32.8 jit_solution(15383761599996038137)
XLA Ops:
  0.7 31.4 %cycle.1 = f32[3,64,768]{2,1,0:T(8,128)S(1)} custom-call(f32[3,64,768]{2,1,0:T(8,128)} %bitcast.4, f32[3,64,768]{2,1,0:T(8,128)} %bitcast.5, s32[1]{0:T(128)S(6)} %copy.6.anc_ref, s32[128,768]{1,0:T(8,128)} %bath_ref.1), custom_call_target="tpu_custom_call" | custom-call | tf_op jit(solution)/shard_map/cycle/pallas_call | solution.py:381
  32.0 0.8 %copy.7 = f32[1,3,64,768]{3,2,1,0:T(8,128)} copy(f32[1,3,64,768]{3,2,1,0:T(8,128)S(1)} %bitcast.3) | data formatting | bytes 1179648
where the time goes:
time: 33 us; the launch traced here: 32.8 us
  Pallas kernels  31.4 us (95%)
  local copies, waits for them, and re-layouts  0.82 us (2%)
  between operations  0.66 us (2%)
    pallas_call x1, Pallas kernels, cycle(): pl.pallas_call(functools.partial(cycle_kernel, n, pair, rows, cols), out_...  31.4 us
    unnamed x1, local copies, waits for them, and re-layouts  0.82 us

commit v1 on v0

--- a/solution.py
+++ b/solution.py
@@ -146,17 +146,6 @@
     def on(level, k):
         return (level * pair + (y + k // pair) % pair) * pair + (x + k % pair) % pair
 
-    @pl.when(hub)
-    def _():
-        def greet(t, carry):
-            to = lax.rem(me + 1 + t, n)
-            pl.semaphore_signal(barrier, inc=1, device_id={"ens": to}, device_id_type=MESH)
-            return carry
-
-        lax.fori_loop(0, n - 1, greet, 0)
-
-    pl.semaphore_signal(barrier, inc=1, device_id={"slab": 1 - s}, device_id_type=MESH)
-
     inner = pl.multiple_of((1 - s) * (rows - 2 * STRIP), STRIP)
     fills = [
         pltpu.make_async_copy(src, dst, loads.at[i])
@@ -174,6 +163,17 @@
     ]
     for fill in fills:
         fill.start()
+    @pl.when(hub)
+    def _():
+        def greet(t, carry):
+            to = lax.rem(me + n - 1 - t, n)
+            pl.semaphore_signal(barrier, inc=1, device_id={"ens": to}, device_id_type=MESH)
+            return carry
+
+        lax.fori_loop(0, n - 1, greet, 0)
+
+    pl.semaphore_signal(barrier, inc=1, device_id={"slab": 1 - s}, device_id_type=MESH)
+
 
     lin_v[me] = jnp.full((1, LANES), anc_ref[0], jnp.int32)
     zeros = jnp.zeros((STRIP, cols), jnp.float32)
@@ -215,16 +215,24 @@
         northward = (shifted(h, r, 1) - shifted(h, r, -1)) * 0.5
         cells[2, here] = v - RATIO * northward - TURNING * u
 
-    for step in range(STEPS):
-        for r in range(top, bottom, STRIP):
-            heights(state, sb, r)
-        for r in range(top, bottom, STRIP):
-            velocities(state, r)
+    def sweep(first, past):
+        for wave in range(first, past):
+            for step in range(STEPS):
+                r = top + (wave - 2 * step) * STRIP
+                if top <= r < bottom:
+                    heights(state, sb, r)
+                if top <= r - STRIP < bottom:
+                    velocities(state, r - STRIP)
+
+    half = plane + 2 * (STEPS - 1)
+    early = z >= line // 2
+    sweep(0, half)
+    pl.when(jnp.logical_not(early))(lambda: sweep(half, half + plane + 1))
 
     edge = pl.multiple_of((1 - s) * (rows - STRIP), STRIP)
 
     def strip(ref, f, q, offset):
-        return ref.at[f, pl.ds(pl.multiple_of(offset + (q + s * (hubs - 1 - 2 * q)) * STRIP, STRIP), STRIP)]
+        return ref.at[f, pl.ds(pl.multiple_of(offset + q * STRIP, STRIP), STRIP)]
 
     def deliver(f, to):
         pltpu.make_async_remote_copy(
@@ -252,18 +260,22 @@
     side = line // 2 - 1 + z // (line // 2)
     targets = [on(side + inward, k) for k in reversed(range(plane))]
     targets += [on(side, k) for k in reversed(range(plane))]
-    last_hub = base + hubs - 1
-
-    def away(f):
-        for to in targets[:-1]:
-            pl.when(to != last_hub)(lambda to=to: deliver(f, to))
+    seam_hub = base + (1 - s) * (hubs - 1)
+
+    def across(f):
+        for to in targets[:plane]:
+            pl.when(to != seam_hub)(lambda to=to: deliver(f, to))
+
+    def along(f):
+        for to in targets[plane:-1]:
+            pl.when(to != seam_hub)(lambda to=to: deliver(f, to))
         to = targets[-1]
-        pl.when(jnp.logical_and(jnp.logical_not(hub), to != last_hub))(lambda: deliver(f, to))
-        pl.when(jnp.logical_and(hub, to != last_hub))(lambda: keep(f))
+        pl.when(jnp.logical_and(jnp.logical_not(hub), to != seam_hub))(lambda: deliver(f, to))
+        pl.when(jnp.logical_and(hub, to != seam_hub))(lambda: keep(f))
 
     def seamed(f):
-        pl.when(me != last_hub)(lambda: deliver(f, last_hub))
-        pl.when(me == last_hub)(lambda: keep(f))
+        pl.when(me != seam_hub)(lambda: deliver(f, seam_hub))
+        pl.when(me == seam_hub)(lambda: keep(f))
 
     pl.semaphore_wait(barrier, hubs + 1 - hub.astype(jnp.int32))
     halos = []
@@ -283,7 +295,13 @@
     for to in targets[:-1]:
         tell(to)
     pl.when(jnp.logical_not(hub))(lambda: tell(targets[-1]))
-    away(0)
+    @pl.when(early)
+    def _():
+        across(0)
+        sweep(half, half + plane + 1)
+
+    pl.when(jnp.logical_not(early))(lambda: across(0))
+    along(0)
     halos[0].wait()
     for step in range(STEPS):
         last = step == STEPS - 1
@@ -296,7 +314,9 @@
 
     seamed(0)
     for f in (1, 2):
-        away(f)
+        pl.when(s == 0)(lambda f=f: across(f))
+        along(f)
+        pl.when(s == 1)(lambda f=f: across(f))
         seamed(f)
 
     wall = pl.multiple_of(s * (rows + STRIP), STRIP)

time: 33 us -> 32.4 us (0.982)
  Pallas kernels: 31.4 us -> 30.7 us
    pallas_call x1, Pallas kernels: 31.4 us -> 30.7 us  [cycle(): pl.pallas_call(functools.partial(cycle_kernel, n, pair, rows, cols), out_...]
where the time goes in v1:
time: 32.4 us; the launch traced here: 32.2 us
  Pallas kernels  30.7 us (95%)
  local copies, waits for them, and re-layouts  0.82 us (3%)
  between operations  0.66 us (2%)
    pallas_call x1, Pallas kernels, cycle(): pl.pallas_call(functools.partial(cycle_kernel, n, pair, rows, cols), out_...  30.7 us
    unnamed x1, local copies, waits for them, and re-layouts  0.82 us

profile of v1, /device:TPU:8, one launch (start us, length us, event | category | flops | bytes accessed | tf_op | source)
XLA Modules:
  0.0 32.2 jit_solution(14272283775103874098)
XLA Ops:
  0.7 30.7 %cycle.1 = f32[3,64,768]{2,1,0:T(8,128)S(1)} custom-call(f32[3,64,768]{2,1,0:T(8,128)} %bitcast.4, f32[3,64,768]{2,1,0:T(8,128)} %bitcast.5, s32[1]{0:T(128)S(6)} %copy.6.anc_ref, s32[128,768]{1,0:T(8,128)} %bath_ref.1), custom_call_target="tpu_custom_call" | custom-call | tf_op jit(solution)/shard_map/cycle/pallas_call | solution.py:401
  31.4 0.8 %copy.7 = f32[1,3,64,768]{3,2,1,0:T(8,128)} copy(f32[1,3,64,768]{3,2,1,0:T(8,128)S(1)} %bitcast.3) | data formatting | bytes 1179648

commit v2 on v1

--- a/solution.py
+++ b/solution.py
@@ -16,6 +16,7 @@
 RATIO = 0.3
 TURNING = 0.03
 JITTER = 0.5
+SLOPE = RATIO * 0.5
 
 
 def padded(cells, sides, width):
@@ -123,7 +124,7 @@
 def cycle_kernel(
     n, pair, rows, cols,
     ens_ref, pert_ref, anc_ref, bath_ref, out_ref,
-    state, noise, sb, seam, seam_sb, bath_v, pieces0, pieces1, pieces2, picked, res, lin_v, lin_s,
+    state, noise, sb, flux, seam, seam_sb, seam_flux, bath_v, pieces0, pieces1, pieces2, picked, res, lin_v, lin_s,
     halo_send, halo_recv, lin_send, lin_recv, lin_local, loads,
     a_send, a_recv, b_send, b_recv,
 ):
@@ -165,12 +166,12 @@
         fill.start()
     @pl.when(hub)
     def _():
-        def greet(t, carry):
-            to = lax.rem(me + n - 1 - t, n)
-            pl.semaphore_signal(barrier, inc=1, device_id={"ens": to}, device_id_type=MESH)
-            return carry
-
-        lax.fori_loop(0, n - 1, greet, 0)
+        side = line // 2 - 1 + z // (line // 2)
+        for level in (side + inward, side, side - inward, side + 2 * inward):
+            for k in reversed(range(plane)):
+                to = on(level, k)
+                if level is not side or k:
+                    pl.semaphore_signal(barrier, inc=1, device_id={"ens": to}, device_id_type=MESH)
 
     pl.semaphore_signal(barrier, inc=1, device_id={"slab": 1 - s}, device_id_type=MESH)
 
@@ -178,51 +179,57 @@
     lin_v[me] = jnp.full((1, LANES), anc_ref[0], jnp.int32)
     zeros = jnp.zeros((STRIP, cols), jnp.float32)
     for r in (0, bottom):
-        sb[r : r + STRIP] = zeros
-        for f in range(3):
-            state[f, r : r + STRIP] = zeros
+        flux[r : r + STRIP] = zeros
+        state[0, r : r + STRIP] = zeros
     fills[0].wait()
     for r in range(0, rows, STRIP):
         depth = bath_v[pl.ds(pl.multiple_of(s * STRIP + r, STRIP), STRIP)]
-        sb[top + r : top + r + STRIP] = depth.astype(jnp.float32) * 0.01
+        sb[top + r : top + r + STRIP] = depth.astype(jnp.float32) * (0.01 * SLOPE)
     for r in range(0, 3 * STRIP, STRIP):
         depth = bath_v[pl.ds(pl.multiple_of((1 - s) * (rows - 2 * STRIP) + r, STRIP), STRIP)]
-        seam_sb[r : r + STRIP] = depth.astype(jnp.float32) * 0.01
+        seam_sb[r : r + STRIP] = depth.astype(jnp.float32) * (0.01 * SLOPE)
     fills[1].wait()
     fills[2].wait()
 
     def east(x):
-        return (pltpu.roll(x, cols - 1, 1) - pltpu.roll(x, 1, 1)) * 0.5
-
-    def shifted(ref, r, by):
-        if 0 <= r + by <= ref.shape[0] - STRIP:
-            return ref[r + by : r + by + STRIP]
-        return pltpu.roll(ref[r : r + STRIP], -by % STRIP, 0)
-
-    def heights(cells, floor, r):
+        return pltpu.roll(x, cols - 1, 1) - pltpu.roll(x, 1, 1)
+
+    def north(ref, r):
+        above = ref.shape[0] - STRIP
+        up = ref[r + 1 : r + 1 + STRIP] if r < above else pltpu.roll(ref[r : r + STRIP], STRIP - 1, 0)
+        down = ref[r - 1 : r - 1 + STRIP] if r else pltpu.roll(ref[r : r + STRIP], 1, 0)
+        return up - down
+
+    def fluxes(cells, floor, flow, r):
         here = slice(r, r + STRIP)
-        v = cells.at[2]
-        northward = shifted(floor, r, 1) * shifted(v, r, 1) - shifted(floor, r, -1) * shifted(v, r, -1)
-        eastward = east(floor[here] * cells[1, here])
-        cells[0, here] = cells[0, here] - RATIO * (eastward + northward * 0.5)
-
-    def velocities(cells, r):
+        flow[here] = floor[here] * cells[2, here]
+
+    def heights(cells, floor, flow, r):
+        here = slice(r, r + STRIP)
+        cells[0, here] = cells[0, here] - (east(floor[here] * cells[1, here]) + north(flow, r))
+
+    def velocities(cells, floor, flow, r, last):
         here = slice(r, r + STRIP)
         u = cells[1, here]
         v = cells[2, here]
         h = cells.at[0]
-        cells[1, here] = u - RATIO * east(h[here]) + TURNING * v
-        northward = (shifted(h, r, 1) - shifted(h, r, -1)) * 0.5
-        cells[2, here] = v - RATIO * northward - TURNING * u
+        cells[1, here] = u - SLOPE * east(h[here]) + TURNING * v
+        v = v - SLOPE * north(h, r) - TURNING * u
+        cells[2, here] = v
+        if not last:
+            flow[here] = floor[here] * v
+
+    for r in range(top, bottom, STRIP):
+        fluxes(state, sb, flux, r)
 
     def sweep(first, past):
         for wave in range(first, past):
             for step in range(STEPS):
                 r = top + (wave - 2 * step) * STRIP
                 if top <= r < bottom:
-                    heights(state, sb, r)
+                    heights(state, sb, flux, r)
                 if top <= r - STRIP < bottom:
-                    velocities(state, r - STRIP)
+                    velocities(state, sb, flux, r - STRIP, step == STEPS - 1)
 
     half = plane + 2 * (STEPS - 1)
     early = z >= line // 2
@@ -302,22 +309,25 @@
 
     pl.when(jnp.logical_not(early))(lambda: across(0))
     along(0)
+    across(1)
     halos[0].wait()
+    for r in range(0, 3 * STRIP, STRIP):
+        fluxes(seam, seam_sb, seam_flux, r)
     for step in range(STEPS):
         last = step == STEPS - 1
         for r in range(0, 3 * STRIP, STRIP):
-            heights(seam, seam_sb, r)
+            heights(seam, seam_sb, seam_flux, r)
         for r in range(STRIP, 2 * STRIP, STRIP) if last else range(0, 3 * STRIP, STRIP):
-            velocities(seam, r)
+            velocities(seam, seam_sb, seam_flux, r, last)
     for f in range(3):
         state[f, pl.ds(pl.multiple_of(top + edge, STRIP), STRIP)] = seam[f, STRIP : 2 * STRIP]
 
     seamed(0)
-    for f in (1, 2):
-        pl.when(s == 0)(lambda f=f: across(f))
-        along(f)
-        pl.when(s == 1)(lambda f=f: across(f))
-        seamed(f)
+    along(1)
+    seamed(1)
+    across(2)
+    along(2)
+    seamed(2)
 
     wall = pl.multiple_of(s * (rows + STRIP), STRIP)
     for f in range(3):
@@ -353,18 +363,28 @@
                 device_id_type=MESH,
             ).start()
 
-        for stage in range(3 + line // 2 - 1):
+        for stage in range(3 + line // 2):
             if stage < 3:
                 whole_wait(pieces[stage], a_recv.at[stage])
-            for i, (t, k) in enumerate(spots):
-                f = stage - max(line // 2 - t, 0) if t > 0 else stage
-                if 0 <= f < 3:
-                    reply(f, i)
+            def batch(order, lag, stage=stage):
+                for t in order:
+                    f = stage - lag[t]
+                    for i, (level, k) in enumerate(spots):
+                        if level == t and 0 <= f < 3 and (f < 1 or level != 1):
+                            reply(f, i)
+
+            pl.when(s == 0)(lambda: batch([2, 1, -1, 0], {2: 0, 1: 1, -1: 0, 0: 0}))
+            pl.when(s == 1)(lambda: batch([-1, 0, 2, 1], {2: 1, 1: 2, -1: 0, 0: 0}))
             if stage < 3:
                 picked[stage, n - 1] = pieces[stage][lin_s[me, 0, 0]]
                 pltpu.make_async_copy(
                     picked.at[stage, n - 1], strip(res, stage, me - base, 0), b_recv.at[stage]
                 ).start()
+
+        for i, (level, k) in enumerate(spots):
+            for f in (1, 2):
+                if level == 1:
+                    reply(f, i)
 
     pl.when(hub)(serve)
 
@@ -407,7 +427,9 @@
             pltpu.VMEM((3, tall, cols), f32),
             pltpu.VMEM((3, tall, cols), f32),
             pltpu.VMEM((tall, cols), f32),
+            pltpu.VMEM((tall, cols), f32),
             pltpu.VMEM((3, 3 * STRIP, cols), f32),
+            pltpu.VMEM((3 * STRIP, cols), f32),
             pltpu.VMEM((3 * STRIP, cols), f32),
             pltpu.VMEM((rows + STRIP, cols), jnp.int32),
             pltpu.VMEM((n, STRIP, cols), f32),

time: 32.4 us -> 31.9 us (0.985)
  Pallas kernels: 30.7 us -> 30.2 us
    pallas_call x1, Pallas kernels: 30.7 us -> 30.2 us  [cycle(): pl.pallas_call(functools.partial(cycle_kernel, n, pair, rows, cols), out_...]
where the time goes in v2:
time: 31.9 us; the launch traced here: 31.6 us
  Pallas kernels  30.2 us (95%)
  local copies, waits for them, and re-layouts  0.82 us (3%)
  between operations  0.66 us (2%)
    pallas_call x1, Pallas kernels, cycle(): pl.pallas_call(functools.partial(cycle_kernel, n, pair, rows, cols), out_...  30.2 us
    unnamed x1, local copies, waits for them, and re-layouts  0.82 us

profile of v2, /device:TPU:8, one launch (start us, length us, event | category | flops | bytes accessed | tf_op | source)
XLA Modules:
  0.0 31.6 jit_solution(14832477755545890792)
XLA Ops:
  0.7 30.2 %cycle.1 = f32[3,64,768]{2,1,0:T(8,128)S(1)} custom-call(f32[3,64,768]{2,1,0:T(8,128)} %bitcast.4, f32[3,64,768]{2,1,0:T(8,128)} %bitcast.5, s32[1]{0:T(128)S(6)} %copy.6.anc_ref, s32[128,768]{1,0:T(8,128)} %bath_ref.1), custom_call_target="tpu_custom_call" | custom-call | tf_op jit(solution)/shard_map/cycle/pallas_call | solution.py:421
  30.8 0.8 %copy.7 = f32[1,3,64,768]{3,2,1,0:T(8,128)} copy(f32[1,3,64,768]{3,2,1,0:T(8,128)S(1)} %bitcast.3) | data formatting | bytes 1179648

commit v3 on v2

--- a/solution.py
+++ b/solution.py
@@ -358,7 +358,7 @@
                 src_ref=picked.at[f, i],
                 dst_ref=strip(res, f, me - base, 0),
                 send_sem=b_send.at[f],
-                recv_sem=b_recv.at[f],
+                recv_sem=b_recv.at[f, (me - base) // plane],
                 device_id={"ens": to},
                 device_id_type=MESH,
             ).start()
@@ -378,7 +378,7 @@
             if stage < 3:
                 picked[stage, n - 1] = pieces[stage][lin_s[me, 0, 0]]
                 pltpu.make_async_copy(
-                    picked.at[stage, n - 1], strip(res, stage, me - base, 0), b_recv.at[stage]
+                    picked.at[stage, n - 1], strip(res, stage, me - base, 0), b_recv.at[stage, (me - base) // plane]
                 ).start()
 
         for i, (level, k) in enumerate(spots):
@@ -388,10 +388,14 @@
 
     pl.when(hub)(serve)
 
+    near = z // (line // 2)
     for f in range(3):
-        whole_wait(res.at[f], b_recv.at[f])
-        for r in range(0, rows, STRIP):
-            out_ref[f, r : r + STRIP] = res[f, r : r + STRIP] + out_ref[f, r : r + STRIP]
+        for half in (near, 1 - near):
+            start = half * plane * STRIP
+            whole_wait(res.at[f, pl.ds(pl.multiple_of(start, STRIP), plane * STRIP)], b_recv.at[f, half])
+            for q in range(plane):
+                here = pl.ds(pl.multiple_of(start + q * STRIP, STRIP), STRIP)
+                out_ref[f, here] = res[f, here] + out_ref[f, here]
 
     @pl.when(hub)
     def _():
@@ -440,7 +444,7 @@
             pltpu.VMEM((n, 1, LANES), jnp.int32),
             pltpu.SMEM((n, 1, LANES), jnp.int32),
             dma((2,)), dma((2,)), dma(()), dma(()), dma(()), dma((4,)),
-            dma((3,)), dma((3,)), dma((3,)), dma((3,)),
+            dma((3,)), dma((3,)), dma((3,)), dma((3, 2)),
         ],
         compiler_params=pltpu.CompilerParams(collective_id=0, has_side_effects=True, vmem_limit_bytes=24 << 20),
         name="cycle",

time: 31.9 us -> 31.9 us (level)
  no operation moved by 1% of the time
where the time goes in v3:
time: 31.9 us; the launch traced here: 31.6 us
  Pallas kernels  30.2 us (95%)
  local copies, waits for them, and re-layouts  0.82 us (3%)
  between operations  0.66 us (2%)
    pallas_call x1, Pallas kernels, cycle(): pl.pallas_call(functools.partial(cycle_kernel, n, pair, rows, cols), out_...  30.2 us
    unnamed x1, local copies, waits for them, and re-layouts  0.82 us

profile of v3, /device:TPU:8, one launch (start us, length us, event | category | flops | bytes accessed | tf_op | source)
XLA Modules:
  0.0 31.6 jit_solution(1492363666493677062)
XLA Ops:
  0.7 30.2 %cycle.1 = f32[3,64,768]{2,1,0:T(8,128)S(1)} custom-call(f32[3,64,768]{2,1,0:T(8,128)} %bitcast.4, f32[3,64,768]{2,1,0:T(8,128)} %bitcast.5, s32[1]{0:T(128)S(6)} %copy.6.anc_ref, s32[128,768]{1,0:T(8,128)} %bath_ref.1), custom_call_target="tpu_custom_call" | custom-call | tf_op jit(solution)/shard_map/cycle/pallas_call | solution.py:425
  30.8 0.8 %copy.7 = f32[1,3,64,768]{3,2,1,0:T(8,128)} copy(f32[1,3,64,768]{3,2,1,0:T(8,128)S(1)} %bitcast.3) | data formatting | bytes 1179648
